TPU v7x, 32 devices: a whole 2x2x4 slice. The times are simulated.
32 devices in a mesh: dp: 8 (over z, x), tensor: 4 (over y, core).
Axes of the slice: x: 2, y: 2, z: 4, core: 2. Of those that a mesh axis runs over, the one named last changes fastest.
Arguments:
- inputs: bfloat16 [8192, 4096], P('dp'), may hold values from -6 to 6
- out_grads: bfloat16 [8192, 6144], P('dp', 'tensor'), may hold values from -0.01953125 to 0.01953125
- left_factor: float32 [4096, 4096], P('dp', 'tensor'), may hold values from -6 to 6
- right_factor: float32 [6144, 6144], P('dp', 'tensor'), may hold values from -6 to 6
- left_basis: float32 [4096, 4096], P('dp', 'tensor'), may hold values from -0.09375 to 0.09375
- right_basis: float32 [6144, 6144], P('dp', 'tensor'), may hold values from -0.078125 to 0.078125
Outputs:
- left_new: float32 [4096, 4096], P('dp', 'tensor')
- right_new: float32 [6144, 6144], P('dp', 'tensor')
- rotated: float32 [4096, 6144], P('dp', 'tensor')
All inputs are finite; a program needn't handle non-finite values.
Results may differ from a plain program's by a relative error of at most 0.019.
Values may be sent and summed in bfloat16 or wider, within the bound.
A program may use at most 192 MiB of HBM per device.

v0:
```python
import jax
import jax.numpy as jnp
from jax import lax
from jax.sharding import PartitionSpec as P

F32 = jnp.float32
BF16 = jnp.bfloat16


def mm(a, b, ca, cb):
    return lax.dot_general(a, b, (((ca,), (cb,)), ((), ())), preferred_element_type=F32)


def spread(block, owner, n_dp, n_t, later):
    me = lax.axis_index("tensor")
    mine = me ^ owner(lax.axis_index("dp"))
    step = n_t // 2
    while step:
        pairs = []
        for d in range(n_dp):
            for k in range(0, n_t, 2 * step):
                src = owner(d) ^ k
                pairs.append((d * n_t + src, d * n_t + (src ^ step)))
        got = lax.ppermute(block, ("dp", "tensor"), pairs)
        if step == n_t // 2:
            got, later = lax.optimization_barrier((got, later))
        block = jnp.where(mine % (2 * step) == step, got, block)
        step //= 2
    return (block, later)


def gather_by_permutes(block, axis, n, hop):
    count = n // hop
    me = lax.axis_index(axis)
    group = me // hop
    got = [block]
    for r in range(1, count):
        pairs = [(p, (p // hop + r) % count * hop + p % hop) for p in range(n)]
        got.append(lax.ppermute(block, axis, pairs))
    return (got, group, count)


def in_order(got, group, count):
    out = jnp.zeros((count,) + got[0].shape, got[0].dtype)
    for r in range(count):
        out = lax.dynamic_update_slice_in_dim(
            out, got[r][None], lax.rem(group - r + count, count), 0
        )
    return out


def shards(inputs, out_grads, left_factor, right_factor, left_basis, right_basis):
    n_dp, n_t = (lax.axis_size("dp"), lax.axis_size("tensor"))
    krows, kcols = left_factor.shape
    mrows, mcols = right_factor.shape
    dp = lax.axis_index("dp")
    right_low = right_basis.astype(BF16)
    left_low = left_basis.astype(BF16)
    zgot, zgroup, zcount = gather_by_permutes(right_low, "dp", n_dp, 2)
    lgot, lgroup, lcount = gather_by_permutes(left_low, "tensor", n_t, 1)
    partial = mm(inputs, out_grads, 0, 0).astype(BF16)
    summed = lax.psum_scatter(partial, "dp", scatter_dimension=0, tiled=True)
    left_rows = in_order(lgot, lgroup, lcount)
    left_cols = lax.all_to_all(
        left_rows.reshape(n_t, krows, kcols // krows, krows)
        .transpose(0, 2, 1, 3)
        .reshape(n_dp, krows, krows),
        "dp",
        split_axis=0,
        concat_axis=0,
        tiled=True,
    ).reshape(n_dp * krows, krows)
    cross = [(p, p ^ 1) for p in range(n_dp)]
    early = len(zgot) // 2
    first = [lax.ppermute(z, "dp", cross) for z in zgot[:early]]
    summed, zgot, first, left_cols = lax.optimization_barrier((summed, zgot, first, left_cols))
    col_panel = lax.all_gather(summed, "dp", axis=0, tiled=True)
    last = [lax.ppermute(z, "dp", cross) for z in zgot[early:]]
    basis_panel = jnp.zeros((n_dp,) + right_low.shape, BF16)
    for r in range(early):
        at = lax.rem(zgroup - r + zcount, zcount) * 2 + lax.rem(dp, 2)
        basis_panel = lax.dynamic_update_slice_in_dim(basis_panel, zgot[r][None], at, 0)
        basis_panel = lax.dynamic_update_slice_in_dim(basis_panel, first[r][None], at ^ 1, 0)
    col_panel, last, basis_panel = lax.optimization_barrier((col_panel, last, basis_panel))
    for r in range(early, zcount):
        at = lax.rem(zgroup - r + zcount, zcount) * 2 + lax.rem(dp, 2)
        basis_panel = lax.dynamic_update_slice_in_dim(basis_panel, zgot[r][None], at, 0)
        basis_panel = lax.dynamic_update_slice_in_dim(basis_panel, last[r - early][None], at ^ 1, 0)
    basis_panel = basis_panel.reshape(n_dp * mrows, mcols)
    turned = mm(left_cols, col_panel, 0, 0).astype(BF16)
    turned, summed = lax.optimization_barrier((turned, summed))
    turned_rows = lax.all_gather(turned, "tensor", axis=1, tiled=True)
    own = lax.dynamic_slice_in_dim(col_panel, lax.rem(dp * mrows, mcols), mrows, 1)
    parts = jnp.einsum(
        "jkc,rc->jrk", col_panel.reshape(n_t, kcols, mcols), summed, preferred_element_type=F32
    ).astype(BF16)
    own, parts = spread(own, lambda d: d * mrows // mcols, n_dp, n_t, parts)
    gram_left = lax.psum_scatter(
        parts.reshape(n_t * krows, kcols), "tensor", scatter_dimension=0, tiled=True
    ).astype(F32)
    left_new = 0.95 * left_factor + 0.05 * gram_left
    right_new = 0.95 * right_factor + 0.05 * mm(own, col_panel, 0, 0)
    rotated = mm(turned_rows, basis_panel, 1, 0)
    return (left_new, right_new, rotated)


def solution(mesh):
    spec = P("dp", "tensor")
    return jax.shard_map(
        shards,
        mesh=mesh,
        in_specs=(P("dp", None), spec, spec, spec, spec, spec),
        out_specs=(spec, spec, spec),
        check_vma=False,
    )
```

profile of v0, /device:TPU:25, one launch (start us, length us, event | category | flops | bytes accessed | tf_op | source)
XLA Modules:
  0.0 908.6 jit_solution(4041019502134151689)
XLA Ops:
  9.1 19.2 %convolution_convert_fusion = bf16[4096,1536]{1,0:T(8,128)(2,1)} fusion(bf16[1024,4096]{1,0:T(8,128)(2,1)} %param.6, bf16[1024,1536]{1,0:T(8,128)(2,1)S(1)} %copy-done), kind=kOutput, calls=%fused_computation | convolution fusion | flops 12891193344 | bytes 24117248 | tf_op jit(solution)/shard_map/dot_general | solution.py:11
  34.3 22.0 %collective-permute-done.5 = bf16[512,1024]{1,0:T(8,128)(2,1)} collective-permute-done((bf16[512,1024]{1,0:T(8,128)(2,1)S(1)}, bf16[512,1024]{1,0:T(8,128)(2,1)}, u32[]{:S(2)}, u32[]{:S(2)}) %collective-permute-start.5) | collective-permute-done | bytes 1048608 | tf_op jit(solution)/shard_map/ppermute | solution.py:39
  58.6 21.3 %collective-permute-done.6 = bf16[512,1024]{1,0:T(8,128)(2,1)S(1)} collective-permute-done((bf16[512,1024]{1,0:T(8,128)(2,1)S(1)}, bf16[512,1024]{1,0:T(8,128)(2,1)S(1)}, u32[]{:S(2)}, u32[]{:S(2)}) %collective-permute-start.6) | collective-permute-done | bytes 1048608 | tf_op jit(solution)/shard_map/ppermute | solution.py:39
  86.8 5.6 all-to-all-start
  92.3 2.6 convert_element_type.22
  97.9 159.0 %collective-permute-done = bf16[768,1536]{1,0:T(8,128)(2,1)S(1)} collective-permute-done((bf16[768,1536]{1,0:T(8,128)(2,1)S(1)}, bf16[768,1536]{1,0:T(8,128)(2,1)S(1)}, u32[]{:S(2)}, u32[]{:S(2)}) %collective-permute-start) | collective-permute-done | bytes 2359328 | tf_op jit(solution)/shard_map/ppermute | solution.py:39
  258.0 224.0 %collective-permute-done.1 = bf16[768,1536]{1,0:T(8,128)(2,1)S(1)} collective-permute-done((bf16[768,1536]{1,0:T(8,128)(2,1)S(1)}, bf16[768,1536]{1,0:T(8,128)(2,1)S(1)}, u32[]{:S(2)}, u32[]{:S(2)}) %collective-permute-start.1) | collective-permute-done | bytes 2359328 | tf_op jit(solution)/shard_map/ppermute | solution.py:39
  487.3 6.8 broadcast_in_dim.47
  500.0 3.3 bitcast_dynamic-update-slice_fusion.4
  503.3 52.1 %collective-permute-done.8 = bf16[768,1536]{1,0:T(8,128)(2,1)} collective-permute-done((bf16[768,1536]{1,0:T(8,128)(2,1)}, bf16[768,1536]{1,0:T(8,128)(2,1)}, u32[]{:S(2)}, u32[]{:S(2)}) %collective-permute-start.8) | collective-permute-done | bytes 2359328 | tf_op jit(solution)/shard_map/ppermute | solution.py:78
  555.4 93.4 %collective-permute-done.9 = bf16[768,1536]{1,0:T(8,128)(2,1)} collective-permute-done((bf16[768,1536]{1,0:T(8,128)(2,1)}, bf16[768,1536]{1,0:T(8,128)(2,1)}, u32[]{:S(2)}, u32[]{:S(2)}) %collective-permute-start.9) | collective-permute-done | bytes 2359328 | tf_op jit(solution)/shard_map/ppermute | solution.py:78
  648.8 60.1 %all-gather.3.cloned.1.call-done = bf16[4096,1536]{1,0:T(8,128)(2,1)} async-done(((bf16[512,1536]{1,0:T(8,128)(2,1)}), bf16[4096,1536]{1,0:T(8,128)(2,1)}) %all-gather.3.cloned.1.call-update) | async-done | bytes 12582928 | tf_op jit(solution)/shard_map/all_gather | solution.py:77
  708.9 11.8 %convolution_convert_fusion.1 = bf16[512,1536]{1,0:T(8,128)(2,1)} fusion(bf16[4096,512]{1,0:T(8,128)(2,1)} %bitcast.5, bf16[4096,1536]{1,0:T(8,128)(2,1)} %all-gather.3.cloned.1.call-done), kind=kOutput, calls=%fused_computation.8 | convolution fusion | flops 6443237376 | bytes 18350080 | tf_op jit(solution)/shard_map/dot_general | solution.py:11
  721.0 9.7 %constant_dynamic-slice_fusion = bf16[4096,768]{1,0:T(8,128)(2,1)} fusion(bf16[4096,1536]{1,0:T(8,128)(2,1)} %all-gather.3.cloned.1.call-done, s32[]{:T(128)S(6)} %select_n.81), kind=kLoop, calls=%fused_computation.23 | loop fusion | bytes 12582916 | tf_op jit(solution)/shard_map/dynamic_slice | solution.py:93
  732.0 19.4 %convert_bitcast_fusion = bf16[4,512,1024]{2,1,0:T(8,128)(2,1)} fusion(bf16[4,1024,1536]{2,1,0:T(8,128)(2,1)} %bitcast.43, bf16[512,1536]{1,0:T(8,128)(2,1)S(1)} %copy-done.10), kind=kOutput, calls=%fused_computation.7 | convolution fusion | flops 6444548096 | bytes 18350080 | tf_op jit(solution)/shard_map/jkc,rc->jrk/dot_general | solution.py:94
  751.4 83.8 %collective-permute-done.10 = bf16[4096,768]{1,0:T(8,128)(2,1)} collective-permute-done((bf16[4096,768]{1,0:T(8,128)(2,1)}, bf16[4096,768]{1,0:T(8,128)(2,1)}, u32[]{:S(2)}, u32[]{:S(2)}) %collective-permute-start.10) | collective-permute-done | bytes 6291488 | tf_op jit(solution)/shard_map/ppermute | solution.py:24
  835.3 12.0 %broadcast_select_fusion = bf16[4096,768]{1,0:T(8,128)(2,1)} fusion(bf16[4096,768]{1,0:T(8,128)(2,1)} %collective-permute-done.10, pred[]{:T(512)S(6)} %eq.10, bf16[4096,1536]{1,0:T(8,128)(2,1)} %all-gather.3.cloned.1.call-done, s32[]{:T(128)S(6)} %select_n.81), kind=kLoop, calls=%fused_computation.3 | loop fusion | flops 3145728 | bytes 18874372 | tf_op jit(solution)/shard_map/jit(_where)/select_n | solution.py:27
  847.2 3.9 collective-permute-start.11
  851.1 3.4 bitcast_dynamic-update-slice_fusion.3
  854.6 3.3 bitcast_dynamic-update-slice_fusion.2
  859.4 3.7 bitcast_dynamic-update-slice_fusion
  863.1 16.9 %fusion.7 = f32[512,1536]{1,0:T(8,128)} fusion(bf16[512,6144]{1,0:T(8,128)(2,1)} %all-gather.5.cloned.1.call-done, bf16[6144,1536]{1,0:T(8,128)(2,1)} %bitcast.18), kind=kOutput, calls=%fused_computation.25 | convolution fusion | flops 9663676416 | bytes 28311552 | tf_op jit(solution)/shard_map/dot_general | solution.py:11
  880.0 18.3 %multiply_add_fusion = f32[768,1536]{1,0:T(8,128)} fusion(f32[768,1536]{1,0:T(8,128)} %param.9, bf16[4096,1536]{1,0:T(8,128)(2,1)} %all-gather.3.cloned.1.call-done, bf16[4096,768]{1,0:T(8,128)(2,1)} %collective-permute-done.11, bf16[4096,768]{1,0:T(8,128)(2,1)} %broadcast_select_fusion, pred[]{:T(512)S(6)} %eq.9), kind=kOutput, calls=%fused_computation.5 | convolution fusion | flops 9670361088 | bytes 34603008 | tf_op jit(solution)/shard_map/dot_general | solution.py:11
  898.3 3.7 multiply_add_fusion.1
  (61 shorter events, 35.4 us)
Async XLA Ops:
  7.2 478.4 %reduce-scatter.3.cloned.1.call-start = ((), (), s32[]{:S(2)}) async-start(), calls=%async_computation.3 | async-start | bytes 14155776 | tf_op jit(solution)/shard_map/reduce_scatter | solution.py:62
  28.2 2.6 copy-start.9
  32.1 24.2 %collective-permute-start.5 = (bf16[512,1024]{1,0:T(8,128)(2,1)S(1)}, bf16[512,1024]{1,0:T(8,128)(2,1)}, u32[]{:S(2)}, u32[]{:S(2)}) collective-permute-start(bf16[512,1024]{1,0:T(8,128)(2,1)S(1)} %get-tuple-element.36), channel_id=1, source_target_pairs={{0,1},{1,2},{2,3},{3,0},{4,5},{5,6},{6,7},{7,4},{8,9},{9,10},{10,1... | collective-permute-start | bytes 3145736 | tf_op jit(solution)/shard_map/ppermute | solution.py:39
  33.9 46.0 %collective-permute-start.6 = (bf16[512,1024]{1,0:T(8,128)(2,1)S(1)}, bf16[512,1024]{1,0:T(8,128)(2,1)S(1)}, u32[]{:S(2)}, u32[]{:S(2)}) collective-permute-start(bf16[512,1024]{1,0:T(8,128)(2,1)S(1)} %get-tuple-element.36), channel_id=1, source_target_pairs={{0,2},{1,3},{2,0},{3,1},{4,6},{5,7},{6,4},{7,5},{8,10},{9,11},{10,... | collective-permute-start | bytes 3145736 | tf_op jit(solution)/shard_map/ppermute | solution.py:39
  34.1 46.8 %collective-permute-start.7 = (bf16[512,1024]{1,0:T(8,128)(2,1)S(1)}, bf16[512,1024]{1,0:T(8,128)(2,1)S(1)}, u32[]{:S(2)}, u32[]{:S(2)}) collective-permute-start(bf16[512,1024]{1,0:T(8,128)(2,1)S(1)} %get-tuple-element.36), channel_id=1, source_target_pairs={{0,3},{1,0},{2,1},{3,2},{4,7},{5,4},{6,5},{7,6},{8,11},{9,8},{10,9... | collective-permute-start | bytes 3145736 | tf_op jit(solution)/shard_map/ppermute | solution.py:39
  86.8 398.8 %all-to-all-start = ((bf16[8,512,512]{2,1,0:T(8,128)(2,1)}), bf16[8,512,512]{2,1,0:T(8,128)(2,1)}, u32[]{:S(2)}, u32[]{:S(2)}) async-start(bf16[8,512,512]{2,1,0:T(8,128)(2,1)} %bitcast.42), calls=%async_computation.1 | async-start | bytes 8388608 | tf_op jit(solution)/shard_map/all_to_all | solution.py:64
  92.3 616.6 %all-gather.3.cloned.1.call-start = ((), (), s32[]{:S(2)}) async-start(), calls=%async_computation.4 | async-start | bytes 14155776 | tf_op jit(solution)/shard_map/all_gather | solution.py:77
  94.9 161.9 %collective-permute-start = (bf16[768,1536]{1,0:T(8,128)(2,1)S(1)}, bf16[768,1536]{1,0:T(8,128)(2,1)S(1)}, u32[]{:S(2)}, u32[]{:S(2)}) collective-permute-start(bf16[768,1536]{1,0:T(8,128)(2,1)S(1)} %convert_element_type.22), channel_id=1, source_target_pairs={{0,8},{4,12},{8,16},{12,20},{16,24},{20,28},{24,0},{28,4},{1,9},{5... | collective-permute-start | bytes 7077896 | tf_op jit(solution)/shard_map/ppermute | solution.py:39
  95.1 386.9 %collective-permute-start.1 = (bf16[768,1536]{1,0:T(8,128)(2,1)S(1)}, bf16[768,1536]{1,0:T(8,128)(2,1)S(1)}, u32[]{:S(2)}, u32[]{:S(2)}) collective-permute-start(bf16[768,1536]{1,0:T(8,128)(2,1)S(1)} %convert_element_type.22), channel_id=1, source_target_pairs={{0,16},{4,20},{8,24},{12,28},{16,0},{20,4},{24,8},{28,12},{1,17},{... | collective-permute-start | bytes 7077896 | tf_op jit(solution)/shard_map/ppermute | solution.py:39
  96.5 385.6 %collective-permute-start.2 = (bf16[768,1536]{1,0:T(8,128)(2,1)S(1)}, bf16[768,1536]{1,0:T(8,128)(2,1)S(1)}, u32[]{:S(2)}, u32[]{:S(2)}) collective-permute-start(bf16[768,1536]{1,0:T(8,128)(2,1)S(1)} %convert_element_type.22), channel_id=1, source_target_pairs={{0,24},{4,28},{8,0},{12,4},{16,8},{20,12},{24,16},{28,20},{1,25},{... | collective-permute-start | bytes 7077896 | tf_op jit(solution)/shard_map/ppermute | solution.py:39
  96.7 385.3 %collective-permute-start.3 = (bf16[768,1536]{1,0:T(8,128)(2,1)S(1)}, bf16[768,1536]{1,0:T(8,128)(2,1)S(1)}, u32[]{:S(2)}, u32[]{:S(2)}) collective-permute-start(bf16[768,1536]{1,0:T(8,128)(2,1)S(1)} %convert_element_type.22), channel_id=1, source_target_pairs={{0,4},{4,0},{8,12},{12,8},{16,20},{20,16},{24,28},{28,24},{1,5},{5... | collective-permute-start | bytes 7077896 | tf_op jit(solution)/shard_map/ppermute | solution.py:75
  256.9 225.2 %copy-start.5 = (bf16[768,1536]{1,0:T(8,128)(2,1)}, bf16[768,1536]{1,0:T(8,128)(2,1)S(1)}, u32[]{:S(2)}) copy-start(bf16[768,1536]{1,0:T(8,128)(2,1)S(1)} %collective-permute-done) | copy-start | bytes 7077892
  256.9 228.7 %collective-permute-start.4 = (bf16[768,1536]{1,0:T(8,128)(2,1)S(1)}, bf16[768,1536]{1,0:T(8,128)(2,1)}, u32[]{:S(2)}, u32[]{:S(2)}) collective-permute-start(bf16[768,1536]{1,0:T(8,128)(2,1)S(1)} %collective-permute-done), channel_id=1, source_target_pairs={{0,4},{4,0},{8,12},{12,8},{16,20},{20,16},{24,28},{28,24},{1,5},{5... | collective-permute-start | bytes 7077896 | tf_op jit(solution)/shard_map/ppermute | solution.py:75
  485.6 377.5 %all-gather.5.cloned.1.call-start = ((), (), s32[]{:S(2)}) async-start(), calls=%async_computation.6 | async-start | bytes 7864320 | tf_op jit(solution)/shard_map/all_gather | solution.py:92
  485.7 69.7 %collective-permute-start.8 = (bf16[768,1536]{1,0:T(8,128)(2,1)}, bf16[768,1536]{1,0:T(8,128)(2,1)}, u32[]{:S(2)}, u32[]{:S(2)}) collective-permute-start(bf16[768,1536]{1,0:T(8,128)(2,1)} %copy-done.4), channel_id=1, source_target_pairs={{0,4},{4,0},{8,12},{12,8},{16,20},{20,16},{24,28},{28,24},{1,5},{5... | collective-permute-start | bytes 7077896 | tf_op jit(solution)/shard_map/ppermute | solution.py:78
  487.2 161.6 %collective-permute-start.9 = (bf16[768,1536]{1,0:T(8,128)(2,1)}, bf16[768,1536]{1,0:T(8,128)(2,1)}, u32[]{:S(2)}, u32[]{:S(2)}) collective-permute-start(bf16[768,1536]{1,0:T(8,128)(2,1)} %copy-done.2), channel_id=1, source_target_pairs={{0,4},{4,0},{8,12},{12,8},{16,20},{20,16},{24,28},{28,24},{1,5},{5... | collective-permute-start | bytes 7077896 | tf_op jit(solution)/shard_map/ppermute | solution.py:78
  494.1 2.8 copy-start.8
  494.1 4.4 copy-start.6
  720.7 177.6 %reduce-scatter.5.cloned.1.call-start = ((), (), s32[]{:S(2)}) async-start(), calls=%async_computation.5 | async-start | bytes 5242880 | tf_op jit(solution)/shard_map/reduce_scatter | solution.py:98
  721.0 11.0 %copy-start.10 = (bf16[512,1536]{1,0:T(8,128)(2,1)S(1)}, bf16[512,1536]{1,0:T(8,128)(2,1)}, u32[]{:S(2)}) copy-start(bf16[512,1536]{1,0:T(8,128)(2,1)} %reduce-scatter.3.cloned.1.call-done) | copy-start | bytes 4718596
  730.7 104.5 %collective-permute-start.10 = (bf16[4096,768]{1,0:T(8,128)(2,1)}, bf16[4096,768]{1,0:T(8,128)(2,1)}, u32[]{:S(2)}, u32[]{:S(2)}) collective-permute-start(bf16[4096,768]{1,0:T(8,128)(2,1)} %constant_dynamic-slice_fusion), channel_id=1, source_target_pairs={{0,2},{4,6},{9,11},{13,15},{18,16},{22,20},{27,25},{31,29}} | collective-permute-start | bytes 18874376 | tf_op jit(solution)/shard_map/ppermute | solution.py:24
  847.2 32.8 %collective-permute-start.11 = (bf16[4096,768]{1,0:T(8,128)(2,1)}, bf16[4096,768]{1,0:T(8,128)(2,1)}, u32[]{:S(2)}, u32[]{:S(2)}) collective-permute-start(bf16[4096,768]{1,0:T(8,128)(2,1)} %broadcast_select_fusion), channel_id=1, source_target_pairs={{0,1},{2,3},{4,5},{6,7},{9,8},{11,10},{13,12},{15,14},{18,19},{16,... | collective-permute-start | bytes 18874376 | tf_op jit(solution)/shard_map/ppermute | solution.py:24
  851.1 6.7 copy-start.3
  880.0 22.1 %copy-start.1 = (bf16[1024,1536]{1,0:T(8,128)(2,1)S(1)}, bf16[1024,1536]{1,0:T(8,128)(2,1)}, u32[]{:S(2)}) copy-start(bf16[1024,1536]{1,0:T(8,128)(2,1)} %param.7) | copy-start | bytes 9437188
  (4 other events, 6.8 us)
Sparse Core Ops, SparseCore 0:
  28.4 407.5 reduce-scatter.2
  485.7 223.0 all-gather.2
  720.9 65.4 all-gather.4
  851.3 44.1 reduce-scatter.4
where the time goes:
time: 909 us
  waiting for transfers between devices  716 us (79%)
  matrix products  85.6 us (9%)
  local copies, waits for them, and re-layouts  52.5 us (6%)
  other arithmetic  21.9 us (2%)
  starting transfers between devices  18.9 us (2%)
  between operations  14 us (2%)
    ppermute x6, waiting for transfers between devices, gather_by_permutes(): got.append(lax.ppermute(block, axis, pairs))  426 us
    ppermute x2, waiting for transfers between devices, shards(): last = [lax.ppermute(z, 'dp', cross) for z in zgot[early:]]  146 us
    ppermute x2, waiting for transfers between devices, spread(): got = lax.ppermute(block, ('dp', 'tensor'), pairs)  83.8 us
    dot_general x4, matrix products, mm(): lax.dot_general(a, b, (((ca,), (cb,)), ((), ())), preferred_element_type=...  66.2 us
    all_gather x1, waiting for transfers between devices, shards(): col_panel = lax.all_gather(summed, 'dp', axis=0, tiled=True)  60.1 us
    dot_general x1, matrix products, shards(): jnp.einsum('jkc,rc->jrk', col_panel.reshape(n_t, kcols, mcols), summed, p...  19.4 us
  transfers between devices with their start and end apart: 17, of which 8 were waited for; matrix products, arithmetic and copies ran while one was open for 13% of the time, Pallas kernels for 0%

commit v1 on v0

--- a/solution.py
+++ b/solution.py
@@ -2,9 +2,24 @@
 import jax.numpy as jnp
 from jax import lax
 from jax.sharding import PartitionSpec as P
+from jax.lax import axis_index, ppermute, psum
 
 F32 = jnp.float32
 BF16 = jnp.bfloat16
+
+
+def masks_number(t0):
+    full_n = psum(1, "dp")
+    trail = list(map(lambda pp: (pp, (pp + 1) % full_n), range(full_n)))
+
+    def _proceed_copies(z_new):
+        if len(z_new) == full_n:
+            return z_new
+        return _proceed_copies([ppermute(z_new[0], "dp", trail), *z_new])
+
+    return jnp.roll(
+        jnp.concatenate(_proceed_copies([t0]), 0), (axis_index("dp") + 1) * t0.shape[0], 0
+    )
 
 
 def mm(a, b, ca, cb):
@@ -74,7 +89,7 @@
     early = len(zgot) // 2
     first = [lax.ppermute(z, "dp", cross) for z in zgot[:early]]
     summed, zgot, first, left_cols = lax.optimization_barrier((summed, zgot, first, left_cols))
-    col_panel = lax.all_gather(summed, "dp", axis=0, tiled=True)
+    col_panel = masks_number(summed)
     last = [lax.ppermute(z, "dp", cross) for z in zgot[early:]]
     basis_panel = jnp.zeros((n_dp,) + right_low.shape, BF16)
     for r in range(early):

time: 909 us -> 1070 us (1.18)
  waiting for transfers between devices: 716 us -> 826 us
  local copies, waits for them, and re-layouts: 52.5 us -> 81.8 us
  starting transfers between devices: 18.9 us -> 42.9 us
    ppermute x0 -> x7, waiting for transfers between devices: none -> 315 us  [_proceed_copies(): return _proceed_copies([ppermute(z_new[0], 'dp', trail), *z_new])]
    ppermute x2, waiting for transfers between devices: 146 us -> 0.01 us  [shards(): last = [lax.ppermute(z, 'dp', cross) for z in zgot[early:]]]
    all_gather x1 -> x0, waiting for transfers between devices: 60.1 us -> none  [shards(): col_panel = lax.all_gather(summed, 'dp', axis=0, tiled=True)]
    unnamed x22 -> x57, local copies, waits for them, and re-layouts: 6.65 us -> 39.4 us
    ppermute x0 -> x7, starting transfers between devices: none -> 20.4 us  [_proceed_copies(): return _proceed_copies([ppermute(z_new[0], 'dp', trail), *z_new])]
  transfers between devices with their start and end apart: 17 -> 23, of which waited for: 8 -> 12; matrix products, arithmetic and copies ran while one was open for 13% -> 13% of each run, Pallas kernels for 0% -> 0%
where the time goes in v1:
time: 1070 us
  waiting for transfers between devices  826 us (77%)
  matrix products  82.8 us (8%)
  local copies, waits for them, and re-layouts  81.8 us (8%)
  starting transfers between devices  42.9 us (4%)
  other arithmetic  21.9 us (2%)
  between operations  14 us (1%)
    ppermute x6, waiting for transfers between devices, gather_by_permutes(): got.append(lax.ppermute(block, axis, pairs))  426 us
    ppermute x7, waiting for transfers between devices, _proceed_copies(): return _proceed_copies([ppermute(z_new[0], 'dp', trail), *z_new])  315 us
    ppermute x2, waiting for transfers between devices, spread(): got = lax.ppermute(block, ('dp', 'tensor'), pairs)  85.1 us
    dot_general x4, matrix products, mm(): lax.dot_general(a, b, (((ca,), (cb,)), ((), ())), preferred_element_type=...  63.8 us
    unnamed x57, local copies, waits for them, and re-layouts  39.4 us
  transfers between devices with their start and end apart: 23, of which 12 were waited for; matrix products, arithmetic and copies ran while one was open for 13% of the time, Pallas kernels for 0%

profile of v1, /device:TPU:25, one launch (start us, length us, event | category | flops | bytes accessed | tf_op | source)
XLA Modules:
  0.0 1069.8 jit_solution(18310904173520489043)
XLA Ops:
  9.1 19.2 %convolution_convert_fusion = bf16[4096,1536]{1,0:T(8,128)(2,1)} fusion(bf16[1024,4096]{1,0:T(8,128)(2,1)} %param.6, bf16[1024,1536]{1,0:T(8,128)(2,1)S(1)} %copy-done), kind=kOutput, calls=%fused_computation | convolution fusion | flops 12891193344 | bytes 24117248 | tf_op jit(solution)/shard_map/dot_general | solution.py:26
  34.4 22.0 %collective-permute-done.5 = bf16[512,1024]{1,0:T(8,128)(2,1)} collective-permute-done((bf16[512,1024]{1,0:T(8,128)(2,1)S(1)}, bf16[512,1024]{1,0:T(8,128)(2,1)}, u32[]{:S(2)}, u32[]{:S(2)}) %collective-permute-start.5) | collective-permute-done | bytes 1048608 | tf_op jit(solution)/shard_map/ppermute | solution.py:54
  58.6 21.3 %collective-permute-done.6 = bf16[512,1024]{1,0:T(8,128)(2,1)S(1)} collective-permute-done((bf16[512,1024]{1,0:T(8,128)(2,1)S(1)}, bf16[512,1024]{1,0:T(8,128)(2,1)S(1)}, u32[]{:S(2)}, u32[]{:S(2)}) %collective-permute-start.6) | collective-permute-done | bytes 1048608 | tf_op jit(solution)/shard_map/ppermute | solution.py:54
  86.8 5.6 all-to-all-start
  98.0 159.0 %collective-permute-done = bf16[768,1536]{1,0:T(8,128)(2,1)S(1)} collective-permute-done((bf16[768,1536]{1,0:T(8,128)(2,1)S(1)}, bf16[768,1536]{1,0:T(8,128)(2,1)S(1)}, u32[]{:S(2)}, u32[]{:S(2)}) %collective-permute-start) | collective-permute-done | bytes 2359328 | tf_op jit(solution)/shard_map/ppermute | solution.py:54
  258.1 224.0 %collective-permute-done.1 = bf16[768,1536]{1,0:T(8,128)(2,1)S(1)} collective-permute-done((bf16[768,1536]{1,0:T(8,128)(2,1)S(1)}, bf16[768,1536]{1,0:T(8,128)(2,1)S(1)}, u32[]{:S(2)}, u32[]{:S(2)}) %collective-permute-start.1) | collective-permute-done | bytes 2359328 | tf_op jit(solution)/shard_map/ppermute | solution.py:54
  487.2 35.3 %collective-permute-done.8 = bf16[512,1536]{1,0:T(8,128)(2,1)S(1)} collective-permute-done((bf16[512,1536]{1,0:T(8,128)(2,1)}, bf16[512,1536]{1,0:T(8,128)(2,1)S(1)}, u32[]{:S(2)}, u32[]{:S(2)}) %collective-permute-start.8) | collective-permute-done | bytes 1572896 | tf_op jit(solution)/shard_map/ppermute | solution.py:18
  524.1 35.0 %collective-permute-done.9 = bf16[512,1536]{1,0:T(8,128)(2,1)S(1)} collective-permute-done((bf16[512,1536]{1,0:T(8,128)(2,1)S(1)}, bf16[512,1536]{1,0:T(8,128)(2,1)S(1)}, u32[]{:S(2)}, u32[]{:S(2)}) %collective-permute-start.9) | collective-permute-done | bytes 1572896 | tf_op jit(solution)/shard_map/ppermute | solution.py:18
  561.1 33.9 %collective-permute-done.10 = bf16[512,1536]{1,0:T(8,128)(2,1)S(1)} collective-permute-done((bf16[512,1536]{1,0:T(8,128)(2,1)S(1)}, bf16[512,1536]{1,0:T(8,128)(2,1)S(1)}, u32[]{:S(2)}, u32[]{:S(2)}) %collective-permute-start.10) | collective-permute-done | bytes 1572896 | tf_op jit(solution)/shard_map/ppermute | solution.py:18
  599.0 30.9 %collective-permute-done.11 = bf16[512,1536]{1,0:T(8,128)(2,1)S(1)} collective-permute-done((bf16[512,1536]{1,0:T(8,128)(2,1)S(1)}, bf16[512,1536]{1,0:T(8,128)(2,1)S(1)}, u32[]{:S(2)}, u32[]{:S(2)}) %collective-permute-start.11) | collective-permute-done | bytes 1572896 | tf_op jit(solution)/shard_map/ppermute | solution.py:18
  631.1 4.9 collective-permute-start.12
  636.0 30.0 %collective-permute-done.12 = bf16[512,1536]{1,0:T(8,128)(2,1)} collective-permute-done((bf16[512,1536]{1,0:T(8,128)(2,1)S(1)}, bf16[512,1536]{1,0:T(8,128)(2,1)}, u32[]{:S(2)}, u32[]{:S(2)}) %collective-permute-start.12) | collective-permute-done | bytes 1572896 | tf_op jit(solution)/shard_map/ppermute | solution.py:18
  670.9 5.0 collective-permute-start.15
  677.9 22.4 %collective-permute-done.13 = bf16[512,1536]{1,0:T(8,128)(2,1)} collective-permute-done((bf16[512,1536]{1,0:T(8,128)(2,1)}, bf16[512,1536]{1,0:T(8,128)(2,1)}, u32[]{:S(2)}, u32[]{:S(2)}) %collective-permute-start.13) | collective-permute-done | bytes 1572896 | tf_op jit(solution)/shard_map/ppermute | solution.py:18
  700.4 4.9 collective-permute-start.14
  707.9 127.3 %collective-permute-done.14 = bf16[512,1536]{1,0:T(8,128)(2,1)S(1)} collective-permute-done((bf16[512,1536]{1,0:T(8,128)(2,1)}, bf16[512,1536]{1,0:T(8,128)(2,1)S(1)}, u32[]{:S(2)}, u32[]{:S(2)}) %collective-permute-start.14) | collective-permute-done | bytes 1572896 | tf_op jit(solution)/shard_map/ppermute | solution.py:18
  861.3 6.1 constant_dynamic-slice_fusion.1
  872.0 9.3 convolution_convert_fusion.1
  881.4 9.6 constant_dynamic-slice_fusion
  892.5 19.0 %convert_bitcast_fusion = bf16[4,512,1024]{2,1,0:T(8,128)(2,1)} fusion(bf16[4,1024,1536]{2,1,0:T(8,128)(2,1)} %bitcast.42, bf16[512,1536]{1,0:T(8,128)(2,1)S(1)} %copy-done.4), kind=kOutput, calls=%fused_computation.7 | convolution fusion | flops 6444548096 | bytes 18350080 | tf_op jit(solution)/shard_map/jkc,rc->jrk/dot_general | solution.py:109
  911.6 85.1 %collective-permute-done.17 = bf16[4096,768]{1,0:T(8,128)(2,1)} collective-permute-done((bf16[4096,768]{1,0:T(8,128)(2,1)}, bf16[4096,768]{1,0:T(8,128)(2,1)}, u32[]{:S(2)}, u32[]{:S(2)}) %collective-permute-start.17) | collective-permute-done | bytes 6291488 | tf_op jit(solution)/shard_map/ppermute | solution.py:39
  996.7 12.0 %broadcast_select_fusion = bf16[4096,768]{1,0:T(8,128)(2,1)} fusion(bf16[4096,768]{1,0:T(8,128)(2,1)} %collective-permute-done.17, pred[]{:T(512)S(6)} %eq.13, bf16[4096,1536]{1,0:T(8,128)(2,1)} %copy-done.2, s32[]{:T(128)S(6)} %select_n.95), kind=kLoop, calls=%fused_computation.3 | loop fusion | flops 3145728 | bytes 18874372 | tf_op jit(solution)/shard_map/jit(_where)/select_n | solution.py:42
  1024.3 17.0 %fusion.7 = f32[512,1536]{1,0:T(8,128)} fusion(bf16[512,6144]{1,0:T(8,128)(2,1)} %all-gather.2.cloned.1.call-done, bf16[6144,1536]{1,0:T(8,128)(2,1)} %bitcast.43), kind=kOutput, calls=%fused_computation.42 | convolution fusion | flops 9663676416 | bytes 28311552 | tf_op jit(solution)/shard_map/dot_general | solution.py:26
  1041.2 18.3 %multiply_add_fusion = f32[768,1536]{1,0:T(8,128)} fusion(f32[768,1536]{1,0:T(8,128)} %param.9, bf16[4096,1536]{1,0:T(8,128)(2,1)} %copy-done.2, bf16[4096,768]{1,0:T(8,128)(2,1)} %collective-permute-done.18, bf16[4096,768]{1,0:T(8,128)(2,1)} %broadcast_select_fusion, pred[]{:T(512)S(6)} %eq.12), kind=kOutput, calls=%fused_computation.5 | convolution fusion | flops 9670361088 | bytes 34603008 | tf_op jit(solution)/shard_map/dot_general | solution.py:26
  (109 shorter events, 98.6 us)
Async XLA Ops:
  7.2 478.5 %reduce-scatter.3.cloned.1.call-start = ((), (), s32[]{:S(2)}) async-start(), calls=%async_computation.3 | async-start | bytes 14155776 | tf_op jit(solution)/shard_map/reduce_scatter | solution.py:77
  32.1 24.2 %collective-permute-start.5 = (bf16[512,1024]{1,0:T(8,128)(2,1)S(1)}, bf16[512,1024]{1,0:T(8,128)(2,1)}, u32[]{:S(2)}, u32[]{:S(2)}) collective-permute-start(bf16[512,1024]{1,0:T(8,128)(2,1)S(1)} %get-tuple-element.36), channel_id=1, source_target_pairs={{0,1},{1,2},{2,3},{3,0},{4,5},{5,6},{6,7},{7,4},{8,9},{9,10},{10,1... | collective-permute-start | bytes 3145736 | tf_op jit(solution)/shard_map/ppermute | solution.py:54
  33.9 46.0 %collective-permute-start.6 = (bf16[512,1024]{1,0:T(8,128)(2,1)S(1)}, bf16[512,1024]{1,0:T(8,128)(2,1)S(1)}, u32[]{:S(2)}, u32[]{:S(2)}) collective-permute-start(bf16[512,1024]{1,0:T(8,128)(2,1)S(1)} %get-tuple-element.36), channel_id=1, source_target_pairs={{0,2},{1,3},{2,0},{3,1},{4,6},{5,7},{6,4},{7,5},{8,10},{9,11},{10,... | collective-permute-start | bytes 3145736 | tf_op jit(solution)/shard_map/ppermute | solution.py:54
  34.1 46.8 %collective-permute-start.7 = (bf16[512,1024]{1,0:T(8,128)(2,1)S(1)}, bf16[512,1024]{1,0:T(8,128)(2,1)S(1)}, u32[]{:S(2)}, u32[]{:S(2)}) collective-permute-start(bf16[512,1024]{1,0:T(8,128)(2,1)S(1)} %get-tuple-element.36), channel_id=1, source_target_pairs={{0,3},{1,0},{2,1},{3,2},{4,7},{5,4},{6,5},{7,6},{8,11},{9,8},{10,9... | collective-permute-start | bytes 3145736 | tf_op jit(solution)/shard_map/ppermute | solution.py:54
  86.8 398.9 %all-to-all-start = ((bf16[8,512,512]{2,1,0:T(8,128)(2,1)}), bf16[8,512,512]{2,1,0:T(8,128)(2,1)}, u32[]{:S(2)}, u32[]{:S(2)}) async-start(bf16[8,512,512]{2,1,0:T(8,128)(2,1)} %bitcast.44), calls=%async_computation.1 | async-start | bytes 8388608 | tf_op jit(solution)/shard_map/all_to_all | solution.py:79
  92.4 931.9 %all-gather.2.cloned.1.call-start = ((), (), s32[]{:S(2)}) async-start(), calls=%async_computation.5 | async-start | bytes 7864320 | tf_op jit(solution)/shard_map/all_gather | solution.py:107
  95.0 162.0 %collective-permute-start = (bf16[768,1536]{1,0:T(8,128)(2,1)S(1)}, bf16[768,1536]{1,0:T(8,128)(2,1)S(1)}, u32[]{:S(2)}, u32[]{:S(2)}) collective-permute-start(bf16[768,1536]{1,0:T(8,128)(2,1)S(1)} %convert_element_type.22), channel_id=1, source_target_pairs={{0,8},{4,12},{8,16},{12,20},{16,24},{20,28},{24,0},{28,4},{1,9},{5... | collective-permute-start | bytes 7077896 | tf_op jit(solution)/shard_map/ppermute | solution.py:54
  95.2 386.9 %collective-permute-start.1 = (bf16[768,1536]{1,0:T(8,128)(2,1)S(1)}, bf16[768,1536]{1,0:T(8,128)(2,1)S(1)}, u32[]{:S(2)}, u32[]{:S(2)}) collective-permute-start(bf16[768,1536]{1,0:T(8,128)(2,1)S(1)} %convert_element_type.22), channel_id=1, source_target_pairs={{0,16},{4,20},{8,24},{12,28},{16,0},{20,4},{24,8},{28,12},{1,17},{... | collective-permute-start | bytes 7077896 | tf_op jit(solution)/shard_map/ppermute | solution.py:54
  96.5 385.6 %collective-permute-start.2 = (bf16[768,1536]{1,0:T(8,128)(2,1)S(1)}, bf16[768,1536]{1,0:T(8,128)(2,1)S(1)}, u32[]{:S(2)}, u32[]{:S(2)}) collective-permute-start(bf16[768,1536]{1,0:T(8,128)(2,1)S(1)} %convert_element_type.22), channel_id=1, source_target_pairs={{0,24},{4,28},{8,0},{12,4},{16,8},{20,12},{24,16},{28,20},{1,25},{... | collective-permute-start | bytes 7077896 | tf_op jit(solution)/shard_map/ppermute | solution.py:54
  96.8 385.3 %collective-permute-start.3 = (bf16[768,1536]{1,0:T(8,128)(2,1)S(1)}, bf16[768,1536]{1,0:T(8,128)(2,1)S(1)}, u32[]{:S(2)}, u32[]{:S(2)}) collective-permute-start(bf16[768,1536]{1,0:T(8,128)(2,1)S(1)} %convert_element_type.22), channel_id=1, source_target_pairs={{0,4},{4,0},{8,12},{12,8},{16,20},{20,16},{24,28},{28,24},{1,5},{5... | collective-permute-start | bytes 7077896 | tf_op jit(solution)/shard_map/ppermute | solution.py:90
  256.9 225.2 %copy-start.16 = (bf16[768,1536]{1,0:T(8,128)(2,1)}, bf16[768,1536]{1,0:T(8,128)(2,1)S(1)}, u32[]{:S(2)}) copy-start(bf16[768,1536]{1,0:T(8,128)(2,1)S(1)} %collective-permute-done) | copy-start | bytes 7077892
  256.9 228.8 %collective-permute-start.4 = (bf16[768,1536]{1,0:T(8,128)(2,1)S(1)}, bf16[768,1536]{1,0:T(8,128)(2,1)}, u32[]{:S(2)}, u32[]{:S(2)}) collective-permute-start(bf16[768,1536]{1,0:T(8,128)(2,1)S(1)} %collective-permute-done), channel_id=1, source_target_pairs={{0,4},{4,0},{8,12},{12,8},{16,20},{20,16},{24,28},{28,24},{1,5},{5... | collective-permute-start | bytes 7077896 | tf_op jit(solution)/shard_map/ppermute | solution.py:90
  485.7 36.7 %collective-permute-start.8 = (bf16[512,1536]{1,0:T(8,128)(2,1)}, bf16[512,1536]{1,0:T(8,128)(2,1)S(1)}, u32[]{:S(2)}, u32[]{:S(2)}) collective-permute-start(bf16[512,1536]{1,0:T(8,128)(2,1)} %reduce-scatter.3.cloned.1.call-done), channel_id=1, source_target_pairs={{0,4},{4,8},{8,12},{12,16},{16,20},{20,24},{24,28},{28,0},{1,5},{5... | collective-permute-start | bytes 4718600 | tf_op jit(solution)/shard_map/ppermute | solution.py:18
  523.6 35.6 %collective-permute-start.9 = (bf16[512,1536]{1,0:T(8,128)(2,1)S(1)}, bf16[512,1536]{1,0:T(8,128)(2,1)S(1)}, u32[]{:S(2)}, u32[]{:S(2)}) collective-permute-start(bf16[512,1536]{1,0:T(8,128)(2,1)S(1)} %collective-permute-done.8), channel_id=1, source_target_pairs={{0,4},{4,8},{8,12},{12,16},{16,20},{20,24},{24,28},{28,0},{1,5},{5... | collective-permute-start | bytes 4718600 | tf_op jit(solution)/shard_map/ppermute | solution.py:18
  560.3 34.6 %collective-permute-start.10 = (bf16[512,1536]{1,0:T(8,128)(2,1)S(1)}, bf16[512,1536]{1,0:T(8,128)(2,1)S(1)}, u32[]{:S(2)}, u32[]{:S(2)}) collective-permute-start(bf16[512,1536]{1,0:T(8,128)(2,1)S(1)} %collective-permute-done.9), channel_id=1, source_target_pairs={{0,4},{4,8},{8,12},{12,16},{16,20},{20,24},{24,28},{28,0},{1,5},{5... | collective-permute-start | bytes 4718600 | tf_op jit(solution)/shard_map/ppermute | solution.py:18
  596.1 33.9 %collective-permute-start.11 = (bf16[512,1536]{1,0:T(8,128)(2,1)S(1)}, bf16[512,1536]{1,0:T(8,128)(2,1)S(1)}, u32[]{:S(2)}, u32[]{:S(2)}) collective-permute-start(bf16[512,1536]{1,0:T(8,128)(2,1)S(1)} %collective-permute-done.10), channel_id=1, source_target_pairs={{0,4},{4,8},{8,12},{12,16},{16,20},{20,24},{24,28},{28,0},{1,5},{5... | collective-permute-start | bytes 4718600 | tf_op jit(solution)/shard_map/ppermute | solution.py:18
  631.1 34.9 %collective-permute-start.12 = (bf16[512,1536]{1,0:T(8,128)(2,1)S(1)}, bf16[512,1536]{1,0:T(8,128)(2,1)}, u32[]{:S(2)}, u32[]{:S(2)}) collective-permute-start(bf16[512,1536]{1,0:T(8,128)(2,1)S(1)} %collective-permute-done.11), channel_id=1, source_target_pairs={{0,4},{4,8},{8,12},{12,16},{16,20},{20,24},{24,28},{28,0},{1,5},{5... | collective-permute-start | bytes 4718600 | tf_op jit(solution)/shard_map/ppermute | solution.py:18
  666.0 34.3 %collective-permute-start.13 = (bf16[512,1536]{1,0:T(8,128)(2,1)}, bf16[512,1536]{1,0:T(8,128)(2,1)}, u32[]{:S(2)}, u32[]{:S(2)}) collective-permute-start(bf16[512,1536]{1,0:T(8,128)(2,1)} %collective-permute-done.12), channel_id=1, source_target_pairs={{0,4},{4,8},{8,12},{12,16},{16,20},{20,24},{24,28},{28,0},{1,5},{5... | collective-permute-start | bytes 4718600 | tf_op jit(solution)/shard_map/ppermute | solution.py:18
  670.9 196.6 %collective-permute-start.15 = (bf16[768,1536]{1,0:T(8,128)(2,1)}, bf16[768,1536]{1,0:T(8,128)(2,1)}, u32[]{:S(2)}, u32[]{:S(2)}) collective-permute-start(bf16[768,1536]{1,0:T(8,128)(2,1)} %copy-done.15), channel_id=1, source_target_pairs={{0,4},{4,0},{8,12},{12,8},{16,20},{20,16},{24,28},{28,24},{1,5},{5... | collective-permute-start | bytes 7077896 | tf_op jit(solution)/shard_map/ppermute | solution.py:93
  675.9 191.6 %collective-permute-start.16 = (bf16[768,1536]{1,0:T(8,128)(2,1)}, bf16[768,1536]{1,0:T(8,128)(2,1)}, u32[]{:S(2)}, u32[]{:S(2)}) collective-permute-start(bf16[768,1536]{1,0:T(8,128)(2,1)} %copy-done.13), channel_id=1, source_target_pairs={{0,4},{4,0},{8,12},{12,8},{16,20},{20,16},{24,28},{28,24},{1,5},{5... | collective-permute-start | bytes 7077896 | tf_op jit(solution)/shard_map/ppermute | solution.py:93
  700.4 134.8 %collective-permute-start.14 = (bf16[512,1536]{1,0:T(8,128)(2,1)}, bf16[512,1536]{1,0:T(8,128)(2,1)S(1)}, u32[]{:S(2)}, u32[]{:S(2)}) collective-permute-start(bf16[512,1536]{1,0:T(8,128)(2,1)} %collective-permute-done.13), channel_id=1, source_target_pairs={{0,4},{4,8},{8,12},{12,16},{16,20},{20,24},{24,28},{28,0},{1,5},{5... | collective-permute-start | bytes 4718600 | tf_op jit(solution)/shard_map/ppermute | solution.py:18
  881.3 178.2 %reduce-scatter.5.cloned.1.call-start = ((), (), s32[]{:S(2)}) async-start(), calls=%async_computation.4 | async-start | bytes 5242880 | tf_op jit(solution)/shard_map/reduce_scatter | solution.py:113
  891.0 105.7 %collective-permute-start.17 = (bf16[4096,768]{1,0:T(8,128)(2,1)}, bf16[4096,768]{1,0:T(8,128)(2,1)}, u32[]{:S(2)}, u32[]{:S(2)}) collective-permute-start(bf16[4096,768]{1,0:T(8,128)(2,1)} %constant_dynamic-slice_fusion), channel_id=1, source_target_pairs={{0,2},{4,6},{9,11},{13,15},{18,16},{22,20},{27,25},{31,29}} | collective-permute-start | bytes 18874376 | tf_op jit(solution)/shard_map/ppermute | solution.py:39
  1008.7 32.5 %collective-permute-start.18 = (bf16[4096,768]{1,0:T(8,128)(2,1)}, bf16[4096,768]{1,0:T(8,128)(2,1)}, u32[]{:S(2)}, u32[]{:S(2)}) collective-permute-start(bf16[4096,768]{1,0:T(8,128)(2,1)} %broadcast_select_fusion), channel_id=1, source_target_pairs={{0,1},{2,3},{4,5},{6,7},{9,8},{11,10},{13,12},{15,14},{18,19},{16,... | collective-permute-start | bytes 18874376 | tf_op jit(solution)/shard_map/ppermute | solution.py:39
  (20 other events, 544.1 us)
Sparse Core Ops, SparseCore 0:
  28.4 407.5 reduce-scatter.2
  881.4 70.9 all-gather.1
  1012.8 45.7 reduce-scatter.4
